TPU v7x, 32 devices: a whole 2x2x4 slice. The times are simulated.
32 devices in a mesh: img: 2 (over y), cls: 4 (over z), emb: 4 (over x, core).
Axes of the slice: x: 2, y: 2, z: 4, core: 2. Of those that a mesh axis runs over, the one named last changes fastest.
Arguments:
- regions: bfloat16 [2048, 1024], P('img', 'emb'), may hold values from -8 to 8
- table: bfloat16 [21504, 1024], P('cls', 'emb'), may hold values from -1 to 1
- shift: float32 [2048], P('img'), may hold values from -0.5 to 0.1
- scale: float32 [2048], P('img'), may hold values from 2 to 20
- labels: int32 [2048], P('img'), may hold values from -1 to 21503, as said below
- valid: int32 [4, 21504], P('img', 'cls'), may hold values 0 or 1
Outputs:
- loss: float32 [], replicated
- region_grad: bfloat16 [2048, 1024], P('img', 'emb')
- table_grad: bfloat16 [21504, 1024], P('cls', 'emb')
Inputs may be any that keep to these rules, and one draw needn't show every extreme that they name: `labels`: -1 marks background; the first region of every image is foreground.
All inputs are finite; a program needn't handle non-finite values. No bound on the sum of `valid` on one device may be relied on, other than what follows from the above.
Results may differ from a plain program's by a relative error of at most 0.0034.
Values may be sent and summed in bfloat16 or wider, within the bound.
A program may use at most 64 MiB of HBM per device.

v0:
```python
import jax
import jax.numpy as jnp
from jax import lax
from jax.sharding import PartitionSpec as P

CLASSES = 21504
REG_IMG = 512


def focal(logit, target):
    prob = jax.nn.sigmoid(logit)
    return -0.25 * target * (1.0 - prob) ** 2 * jax.nn.log_sigmoid(logit) - 0.75 * (
        1.0 - target
    ) * prob**2 * jax.nn.log_sigmoid(-logit)


def shards(regions, table, shift, scale, labels, valid):
    rows = regions.shape[0]
    class_dev = table.shape[0]
    parts = lax.axis_size("emb")
    quarter = rows // parts
    start = lax.axis_index("emb") * quarter
    block = regions.astype(jnp.float32)
    squares = lax.psum(jnp.sum(block * block, axis=1), "emb")
    local_count = jnp.sum((labels >= 0).astype(jnp.float32))
    count = lax.psum(local_count, "img")
    inv = lax.rsqrt(squares + 1e-06)
    unit = block * inv[:, None]
    unit_b = unit.astype(jnp.bfloat16)
    unit_rows = lax.all_to_all(unit_b, "emb", split_axis=0, concat_axis=1, tiled=True)
    cosine = lax.dot_general(
        unit_rows,
        lax.all_gather(table, "emb", axis=1, tiled=True),
        (((1,), (1,)), ((), ())),
        preferred_element_type=jnp.float32,
    )
    shift_q = lax.dynamic_slice_in_dim(shift, start, quarter, 0)
    scale_q = lax.dynamic_slice_in_dim(scale, start, quarter, 0)
    label_q = lax.dynamic_slice_in_dim(labels, start, quarter, 0)
    image_ids = (start + jnp.arange(quarter, dtype=jnp.int32)) // REG_IMG
    onehot = (image_ids[:, None] == jnp.arange(valid.shape[0], dtype=jnp.int32)[None, :]).astype(
        jnp.float32
    )
    mask = jnp.dot(onehot, valid.astype(jnp.float32), preferred_element_type=jnp.float32)
    class_ids = lax.axis_index("cls") * class_dev + jnp.arange(class_dev, dtype=jnp.int32)
    logit = (cosine + shift_q[:, None]) * scale_q[:, None]
    target = (label_q[:, None] == class_ids[None, :]).astype(jnp.float32)
    term, pullback = jax.vjp(lambda value: focal(value, target), logit)
    dlogit = pullback(jnp.ones_like(term))[0]
    total = lax.psum(jnp.sum(term * mask), ("img", "cls", "emb"))
    factor = rows * lax.axis_size("img") / count
    dscore = (dlogit * mask * scale_q[:, None] * factor).astype(jnp.bfloat16)
    piece = lax.all_gather(dscore, "emb", axis=0, tiled=True)
    dunit_piece = jnp.dot(piece, table, preferred_element_type=jnp.float32)
    table_acc = lax.dot_general(
        piece, unit_b, (((0,), (0,)), ((), ())), preferred_element_type=jnp.float32
    )
    dunit = lax.psum(dunit_piece, "cls")
    radial = lax.psum(jnp.sum(unit * dunit, axis=1), "emb")
    region_grad = (inv[:, None] * (dunit - unit * radial[:, None])).astype(jnp.bfloat16)
    table_grad = lax.psum(table_acc, "img").astype(jnp.bfloat16)
    loss = total / count / CLASSES
    return (loss, region_grad, table_grad)


def solution(mesh):
    placed = (P("img", "emb"), P("cls", "emb"), P("img"), P("img"), P("img"), P("img", "cls"))
    return jax.shard_map(
        shards,
        mesh=mesh,
        in_specs=placed,
        out_specs=(P(), P("img", "emb"), P("cls", "emb")),
        check_vma=False,
    )
```

profile of v0, /device:TPU:0, one launch (start us, length us, event | category | flops | bytes accessed | tf_op | source)
XLA Modules:
  0.0 357.9 jit_solution(13751728279272978331)
XLA Ops:
  7.2 0.0 copy-start.2
  7.2 0.0 all-gather.3.cloned.1.call-start
  7.2 0.7 all-gather.3.cloned.1.call-update
  7.9 1.3 fusion.33
  9.2 8.4 %psum.42 = f32[1024]{0:T(1024)S(1)} all-reduce(f32[1024]{0:T(1024)S(1)} %fusion.33), channel_id=1, replica_groups=mesh['img'=2,'cls'=4,'emb'=4] {'emb'}, use_global_device_ids=true, to_apply=%region_1.0 | all-reduce | flops 1024 | bytes 8192 | tf_op jit(solution)/shard_map/psum | solution.py:24
  17.6 1.3 fusion.28
  18.9 1.0 copy.9
  19.9 3.5 all-to-all-start
  23.4 0.0 all-gather.5.cloned.1.call-start
  23.5 0.0 copy-done.2
  23.5 0.6 convert_reduce_fusion
  24.1 5.5 %psum.44 = f32[]{:T(128)} all-reduce(f32[]{:T(128)} %convert_reduce_fusion), channel_id=1, replica_groups=mesh['img'=2,'cls'=4,'emb'=4] {'img'}, use_global_device_ids=true, to_apply=%region_5.7 | all-reduce | flops 1 | bytes 8 | tf_op jit(solution)/shard_map/psum | solution.py:26
  29.6 0.1 dynamic_slice.9
  29.7 0.8 dynamic_slice.11
  30.5 0.8 dynamic_slice.10
  31.9 6.3 %all-to-all-done = bf16[4,256,256]{1,2,0:T(8,128)(2,1)S(1)} async-done(((bf16[4,256,256]{1,2,0:T(8,128)(2,1)}), bf16[4,256,256]{1,2,0:T(8,128)(2,1)S(1)}, u32[]{:S(2)}, u32[]{:S(2)}) %all-to-all-start) | async-done | bytes 524320 | tf_op jit(solution)/shard_map/all_to_all | solution.py:30
  38.2 54.3 %all-gather.3.cloned.1.call-done = bf16[5376,1024]{1,0:T(8,128)(2,1)} async-done(((bf16[5376,256]{1,0:T(8,128)(2,1)}), bf16[5376,1024]{1,0:T(8,128)(2,1)}) %all-gather.3.cloned.1.call-update) | async-done | bytes 11010064 | tf_op jit(solution)/shard_map/all_gather | solution.py:33
  92.5 6.5 %fusion = f32[256,5376]{1,0:T(8,128)S(1)} fusion(bf16[256,1024]{0,1:T(8,128)(2,1)S(1)} %bitcast.11, bf16[5376,1024]{1,0:T(8,128)(2,1)} %all-gather.3.cloned.1.call-done, f32[256]{0:T(256)S(1)} %dynamic_slice.11, f32[256]{0:T(256)S(1)} %dynamic_slice.10), kind=kOutput, calls=%fused_computation.7 | convolution fusion | flops 2821324800 | bytes 17041408 | tf_op jit(solution)/shard_map/dot_general | solution.py:31
  99.1 0.0 copy-start.1
  99.1 18.2 %fusion.12 = (bf16[256,5376]{1,0:T(8,128)(2,1)}, f32[]{:T(128)}) fusion(f32[256,5376]{1,0:T(8,128)S(1)} %fusion, f32[]{:T(128)S(6)} %div.31, f32[256]{0:T(256)S(1)} %dynamic_slice.11, s32[5376]{0:T(1024)S(1)} %iota_add_fusion, s32[256]{0:T(256)S(1)} %dynamic_slice.9, s32[2,5376]{1,0:T(2,128)S(1)} %copy-done.3, s32[256]{0:T(256)S(1)} %and_select_fusion), kind=kOutput, calls=%fused_computation.25 | convolution fusion | flops 94972928 | bytes 8325128 | tf_op jit(solution)/shard_map/dot_general | solution.py:44
  117.3 0.0 all-gather.5.cloned.1.call-update
  117.3 0.0 all-reduce.3.cloned.1.call-start
  117.4 40.5 %psum.43 = f32[]{:T(128)} all-reduce(f32[]{:T(128)} %get-tuple-element.12), channel_id=1, replica_groups=mesh['img'=2,'cls'=4,'emb'=4] {'img','cls','emb'}, use_global_device_ids=true, to_apply=%region_3.5 | all-reduce | flops 1 | bytes 8 | tf_op jit(solution)/shard_map/psum | solution.py:50
  159.2 32.3 %all-gather.5.cloned.1.call-done = bf16[1024,5376]{1,0:T(8,128)(2,1)} async-done(((bf16[256,5376]{1,0:T(8,128)(2,1)}), bf16[1024,5376]{1,0:T(8,128)(2,1)}) %all-gather.5.cloned.1.call-update) | async-done | bytes 11010064 | tf_op jit(solution)/shard_map/all_gather | solution.py:53
  191.5 8.1 %fusion.37 = f32[1024,256]{1,0:T(8,128)} fusion(bf16[1024,5376]{1,0:T(8,128)(2,1)} %all-gather.5.cloned.1.call-done, bf16[5376,256]{1,0:T(8,128)(2,1)S(1)} %copy-done.1), kind=kOutput, calls=%fused_computation.63 | convolution fusion | flops 2818572288 | bytes 14811136 | tf_op jit(solution)/shard_map/dot_general | solution.py:54
  199.6 0.0 all-reduce.3.cloned.1.call-update
  199.7 9.6 %fusion.38 = f32[5376,256]{1,0:T(8,128)} fusion(bf16[1024,5376]{1,0:T(8,128)(2,1)} %all-gather.5.cloned.1.call-done, bf16[1024,256]{1,0:T(8,128)(2,1)S(1)} %fusion.28), kind=kOutput, calls=%fused_computation.64 | convolution fusion | flops 2818572288 | bytes 17039360 | tf_op jit(solution)/shard_map/dot_general | solution.py:55
  209.2 131.1 %all-reduce.4 = bf16[5376,256]{1,0:T(8,128)(2,1)} all-reduce(f32[5376,256]{1,0:T(8,128)} %fusion.38), channel_id=1, replica_groups=mesh['img'=2,'cls'=4,'emb'=4] {'img'}, use_global_device_ids=true, to_apply=%region_9.11 | all-reduce | flops 1376256 | bytes 8257536 | tf_op jit(solution)/shard_map/psum | solution.py:61
  340.4 0.0 copy-done
  340.4 1.6 fusion.29
  342.0 5.9 %psum.46 = f32[1024]{0:T(1024)S(1)} all-reduce(f32[1024]{0:T(1024)S(1)} %fusion.29), channel_id=1, replica_groups=mesh['img'=2,'cls'=4,'emb'=4] {'emb'}, use_global_device_ids=true, to_apply=%region_8.10 | all-reduce | flops 1024 | bytes 8192 | tf_op jit(solution)/shard_map/psum | solution.py:59
  347.9 2.4 fusion.32
  (8 shorter events, 0.0 us)
Async XLA Ops:
  7.2 16.3 %copy-start.2 = (s32[1024]{0:T(1024)S(1)}, s32[1024]{0:T(1024)}, u32[]{:S(2)}) copy-start(s32[1024]{0:T(1024)} %param.11) | copy-start | bytes 12292
  7.2 85.4 %all-gather.3.cloned.1.call-start = ((), (), s32[]{:S(2)}) async-start(), calls=%async_computation.1 | async-start | bytes 13762560 | tf_op jit(solution)/shard_map/all_gather | solution.py:33
  19.9 18.4 %all-to-all-start = ((bf16[4,256,256]{1,2,0:T(8,128)(2,1)}), bf16[4,256,256]{1,2,0:T(8,128)(2,1)S(1)}, u32[]{:S(2)}, u32[]{:S(2)}) async-start(bf16[4,256,256]{1,2,0:T(8,128)(2,1)} %copy.9), calls=%async_computation | async-start | bytes 1048576 | tf_op jit(solution)/shard_map/all_to_all | solution.py:30
  23.4 168.1 %all-gather.5.cloned.1.call-start = ((), (), s32[]{:S(2)}) async-start(), calls=%async_computation.2 | async-start | bytes 13762560 | tf_op jit(solution)/shard_map/all_gather | solution.py:53
  92.5 6.5 %copy-start.3 = (s32[2,5376]{1,0:T(2,128)S(1)}, s32[2,5376]{1,0:T(2,128)}, u32[]{:S(2)}) copy-start(s32[2,5376]{1,0:T(2,128)} %param.12) | copy-start | bytes 129028
  99.1 92.4 %copy-start.1 = (bf16[5376,256]{1,0:T(8,128)(2,1)S(1)}, bf16[5376,256]{1,0:T(8,128)(2,1)}, u32[]{:S(2)}) copy-start(bf16[5376,256]{1,0:T(8,128)(2,1)} %param.8) | copy-start | bytes 8257540
  117.3 223.1 %all-reduce.3.cloned.1.call-start = ((), (), s32[]{:S(2)}) async-start(), calls=%async_computation.3 | async-start | bytes 2097152 | tf_op jit(solution)/shard_map/psum | solution.py:58
  209.2 131.2 %copy-start = (bf16[1024,256]{1,0:T(8,128)(2,1)S(1)}, bf16[1024,256]{1,0:T(8,128)(2,1)}, u32[]{:S(2)}) copy-start(bf16[1024,256]{1,0:T(8,128)(2,1)} %param.7) | copy-start | bytes 1572868
Sparse Core Ops, SparseCore 0:
  9.5 82.9 all-gather.2
  117.4 74.0 all-gather.4
  199.8 51.7 all-reduce.2
where the time goes:
time: 359 us; the launch traced here: 358 us
  blocking collectives  191 us (53%)
  waiting for transfers between devices  93.6 us (26%)
  matrix products  42.4 us (12%)
  between operations  17 us (5%)
  other arithmetic  7.16 us (2%)
  starting transfers between devices  3.66 us (1%)
    psum x1, blocking collectives, shards(): table_grad = lax.psum(table_acc, 'img').astype(jnp.bfloat16)  131 us
    all_gather x1, waiting for transfers between devices, shards(): lax.all_gather(table, 'emb', axis=1, tiled=True)  54.3 us
    psum x1, blocking collectives, shards(): total = lax.psum(jnp.sum(term * mask), ('img', 'cls', 'emb'))  40.5 us
    all_gather x1, waiting for transfers between devices, shards(): piece = lax.all_gather(dscore, 'emb', axis=0, tiled=True)  32.3 us
    dot_general x1, matrix products, shards(): jnp.dot(onehot, valid.astype(jnp.float32), preferred_element_type=jnp.flo...  18.2 us
    dot_general x1, matrix products, shards(): lax.dot_general(piece, unit_b, (((0,), (0,)), ((), ())), preferred_elemen...  9.56 us
    psum x1, blocking collectives, shards(): squares = lax.psum(jnp.sum(block * block, axis=1), 'emb')  8.38 us
    dot_general x1, matrix products, shards(): dunit_piece = jnp.dot(piece, table, preferred_element_type=jnp.float32)  8.13 us
  transfers between devices with their start and end apart: 4, of which 3 were waited for; matrix products, arithmetic and copies ran while one was open for 4% of the time, Pallas kernels for 0%

commit v1 on v0

--- a/solution.py
+++ b/solution.py
@@ -1,3 +1,4 @@
+import functools
 import jax
 import jax.numpy as jnp
 from jax import lax
@@ -5,6 +6,21 @@
 
 CLASSES = 21504
 REG_IMG = 512
+
+
+def mark_streams_on_mesh(inner_x, device_axis, dim_k):
+    return jnp.concatenate(
+        lax.all_to_all(
+            jnp.stack([inner_x for _ in range(lax.axis_size(device_axis))], 0),
+            axis_name=device_axis,
+            split_axis=0,
+            concat_axis=0,
+        ),
+        axis=dim_k,
+    )
+
+
+task_store = functools.partial(mark_streams_on_mesh, device_axis="emb", dim_k=1)
 
 
 def focal(logit, target):
@@ -29,10 +45,7 @@
     unit_b = unit.astype(jnp.bfloat16)
     unit_rows = lax.all_to_all(unit_b, "emb", split_axis=0, concat_axis=1, tiled=True)
     cosine = lax.dot_general(
-        unit_rows,
-        lax.all_gather(table, "emb", axis=1, tiled=True),
-        (((1,), (1,)), ((), ())),
-        preferred_element_type=jnp.float32,
+        unit_rows, task_store(table), (((1,), (1,)), ((), ())), preferred_element_type=jnp.float32
     )
     shift_q = lax.dynamic_slice_in_dim(shift, start, quarter, 0)
     scale_q = lax.dynamic_slice_in_dim(scale, start, quarter, 0)

time: 359 us -> 430 us (1.20)
  waiting for transfers between devices: 93.6 us -> 145 us
  blocking collectives: 191 us -> 203 us
  local copies, waits for them, and re-layouts: 2.61 us -> 8.13 us
    all_to_all x1, waiting for transfers between devices: 6.29 us -> 113 us  [mark_streams_on_mesh(): lax.all_to_all(jnp.stack([inner_x for _ in range(lax.axis_size(device_axi...]
    all_gather x1 -> x0, waiting for transfers between devices: 54.3 us -> none  [shards(): lax.all_gather(table, 'emb', axis=1, tiled=True)]
    all_to_all x0 -> x1, blocking collectives: none -> 11.2 us  [shards(): lax.all_to_all(unit_b, 'emb', split_axis=0, concat_axis=1, tiled=True)]
    another operation x0 -> x1, local copies, waits for them, and re-layouts: none -> 6.52 us  [mark_streams_on_mesh(): jnp.stack([inner_x for _ in range(lax.axis_size(device_axis))], 0)]
  transfers between devices with their start and end apart: 4 -> 3, of which waited for: 3 -> 2; matrix products, arithmetic and copies ran while one was open for 4% -> 3% of each run, Pallas kernels for 0% -> 0%
where the time goes in v1:
time: 430 us; the launch traced here: 429 us
  blocking collectives  203 us (47%)
  waiting for transfers between devices  145 us (34%)
  matrix products  41.9 us (10%)
  between operations  17.3 us (4%)
  local copies, waits for them, and re-layouts  8.13 us (2%)
  other arithmetic  7.09 us (2%)
  starting transfers between devices  6.3 us (1%)
    psum x1, blocking collectives, shards(): table_grad = lax.psum(table_acc, 'img').astype(jnp.bfloat16)  131 us
    all_to_all x1, waiting for transfers between devices, mark_streams_on_mesh(): lax.all_to_all(jnp.stack([inner_x for _ in range(lax.axis_size(device_axi...  113 us
    psum x1, blocking collectives, shards(): total = lax.psum(jnp.sum(term * mask), ('img', 'cls', 'emb'))  40.7 us
    all_gather x1, waiting for transfers between devices, shards(): piece = lax.all_gather(dscore, 'emb', axis=0, tiled=True)  32.4 us
    dot_general x1, matrix products, shards(): jnp.dot(onehot, valid.astype(jnp.float32), preferred_element_type=jnp.flo...  18.2 us
    all_to_all x1, blocking collectives, shards(): lax.all_to_all(unit_b, 'emb', split_axis=0, concat_axis=1, tiled=True)  11.2 us
    dot_general x1, matrix products, shards(): lax.dot_general(piece, unit_b, (((0,), (0,)), ((), ())), preferred_elemen...  9.56 us
  transfers between devices with their start and end apart: 3, of which 2 were waited for; matrix products, arithmetic and copies ran while one was open for 3% of the time, Pallas kernels for 0%

profile of v1, /device:TPU:0, one launch (start us, length us, event | category | flops | bytes accessed | tf_op | source)
XLA Modules:
  0.0 428.7 jit_solution(11291862278960100149)
XLA Ops:
  7.2 1.3 fusion.43
  8.4 8.4 %psum.42 = f32[1024]{0:T(1024)S(1)} all-reduce(f32[1024]{0:T(1024)S(1)} %fusion.43), channel_id=1, replica_groups=mesh['img'=2,'cls'=4,'emb'=4] {'emb'}, use_global_device_ids=true, to_apply=%region_1.0 | all-reduce | flops 1024 | bytes 8192 | tf_op jit(solution)/shard_map/psum | solution.py:40
  16.8 1.2 fusion.38
  18.1 11.2 %all_to_all.21 = bf16[4,256,256]{2,1,0:T(8,128)(2,1)S(1)} all-to-all(bf16[4,256,256]{2,1,0:T(8,128)(2,1)S(1)} %bitcast.23), channel_id=1, replica_groups=mesh['img'=2,'cls'=4,'emb'=4] {'emb'}, dimensions={0} | all-to-all | bytes 1048576 | tf_op jit(solution)/shard_map/all_to_all | solution.py:46
  29.3 6.5 %stack.2 = bf16[4,5376,256]{2,1,0:T(8,128)(2,1)} broadcast(bf16[5376,256]{1,0:T(8,128)(2,1)} %param.8), dimensions={1,2} | broadcast | bytes 13762560 | tf_op jit(solution)/shard_map/stack | solution.py:14
  35.8 6.2 %all-to-all-start.1 = ((bf16[4,5376,256]{2,1,0:T(8,128)(2,1)}), bf16[4,5376,256]{2,1,0:T(8,128)(2,1)}, u32[]{:S(2)}, u32[]{:S(2)}) async-start(bf16[4,5376,256]{2,1,0:T(8,128)(2,1)} %stack.2), calls=%async_computation.1 | async-start | bytes 22020096 | tf_op jit(solution)/shard_map/all_to_all | solution.py:13
  42.0 0.0 all-gather.2.cloned.1.call-start
  42.1 0.0 copy-done.2
  42.1 0.6 convert_reduce_fusion
  42.7 5.5 %psum.44 = f32[]{:T(128)} all-reduce(f32[]{:T(128)} %convert_reduce_fusion), channel_id=1, replica_groups=mesh['img'=2,'cls'=4,'emb'=4] {'img'}, use_global_device_ids=true, to_apply=%region_5.7 | all-reduce | flops 1 | bytes 8 | tf_op jit(solution)/shard_map/psum | solution.py:42
  48.2 0.1 dynamic_slice.9
  48.3 0.8 dynamic_slice.11
  49.1 0.8 dynamic_slice.10
  50.5 0.0 copy-start.3
  50.6 112.7 %all-to-all-done.1 = bf16[4,5376,256]{2,1,0:T(8,128)(2,1)} async-done(((bf16[4,5376,256]{2,1,0:T(8,128)(2,1)}), bf16[4,5376,256]{2,1,0:T(8,128)(2,1)}, u32[]{:S(2)}, u32[]{:S(2)}) %all-to-all-start.1) | async-done | bytes 11010080 | tf_op jit(solution)/shard_map/all_to_all | solution.py:13
  163.3 6.0 %fusion.8 = f32[256,5376]{1,0:T(8,128)S(1)} fusion(bf16[4,5376,256]{2,1,0:T(8,128)(2,1)} %all-to-all-done.1, f32[256]{0:T(256)S(1)} %dynamic_slice.11, f32[256]{0:T(256)S(1)} %dynamic_slice.10, bf16[4,256,256]{2,1,0:T(8,128)(2,1)S(1)} %all_to_all.21), kind=kOutput, calls=%fused_computation.10 | convolution fusion | flops 2821324800 | bytes 17041408 | tf_op jit(solution)/shard_map/dot_general | solution.py:47
  169.2 0.0 copy-done.3
  169.3 0.0 copy-start.1
  169.3 18.2 %fusion.22 = (bf16[256,5376]{1,0:T(8,128)(2,1)}, f32[]{:T(128)}) fusion(f32[256,5376]{1,0:T(8,128)S(1)} %fusion.8, f32[]{:T(128)S(6)} %div.31, f32[256]{0:T(256)S(1)} %dynamic_slice.11, s32[5376]{0:T(1024)S(1)} %iota_add_fusion, s32[256]{0:T(256)S(1)} %dynamic_slice.9, s32[2,5376]{1,0:T(2,128)S(1)} %copy-done.3, s32[256]{0:T(256)S(1)} %and_select_fusion), kind=kOutput, calls=%fused_computation.28 | convolution fusion | flops 94972928 | bytes 8325128 | tf_op jit(solution)/shard_map/dot_general | solution.py:57
  187.5 0.0 all-gather.2.cloned.1.call-update
  187.5 0.0 all-reduce.3.cloned.1.call-start
  187.5 40.7 %psum.43 = f32[]{:T(128)} all-reduce(f32[]{:T(128)} %get-tuple-element.12), channel_id=1, replica_groups=mesh['img'=2,'cls'=4,'emb'=4] {'img','cls','emb'}, use_global_device_ids=true, to_apply=%region_3.5 | all-reduce | flops 1 | bytes 8 | tf_op jit(solution)/shard_map/psum | solution.py:63
  229.6 32.4 %all-gather.2.cloned.1.call-done = bf16[1024,5376]{1,0:T(8,128)(2,1)} async-done(((bf16[256,5376]{1,0:T(8,128)(2,1)}), bf16[1024,5376]{1,0:T(8,128)(2,1)}) %all-gather.2.cloned.1.call-update) | async-done | bytes 11010064 | tf_op jit(solution)/shard_map/all_gather | solution.py:66
  262.0 0.0 copy-done.1
  262.0 8.1 %fusion.48 = f32[1024,256]{1,0:T(8,128)} fusion(bf16[1024,5376]{1,0:T(8,128)(2,1)} %all-gather.2.cloned.1.call-done, bf16[5376,256]{1,0:T(8,128)(2,1)S(1)} %copy-done.1), kind=kOutput, calls=%fused_computation.67 | convolution fusion | flops 2818572288 | bytes 14811136 | tf_op jit(solution)/shard_map/dot_general | solution.py:67
  270.1 0.0 all-reduce.3.cloned.1.call-update
  270.2 9.6 %fusion.49 = f32[5376,256]{1,0:T(8,128)} fusion(bf16[1024,5376]{1,0:T(8,128)(2,1)} %all-gather.2.cloned.1.call-done, bf16[1024,256]{1,0:T(8,128)(2,1)S(1)} %fusion.38), kind=kOutput, calls=%fused_computation.68 | convolution fusion | flops 2818572288 | bytes 17039360 | tf_op jit(solution)/shard_map/dot_general | solution.py:68
  279.7 131.2 %all-reduce.4 = bf16[5376,256]{1,0:T(8,128)(2,1)} all-reduce(f32[5376,256]{1,0:T(8,128)} %fusion.49), channel_id=1, replica_groups=mesh['img'=2,'cls'=4,'emb'=4] {'img'}, use_global_device_ids=true, to_apply=%region_9.11 | all-reduce | flops 1376256 | bytes 8257536 | tf_op jit(solution)/shard_map/psum | solution.py:74
  410.9 0.0 copy-done
  410.9 1.6 fusion.39
  412.5 5.9 %psum.46 = f32[1024]{0:T(1024)S(1)} all-reduce(f32[1024]{0:T(1024)S(1)} %fusion.39), channel_id=1, replica_groups=mesh['img'=2,'cls'=4,'emb'=4] {'emb'}, use_global_device_ids=true, to_apply=%region_8.10 | all-reduce | flops 1024 | bytes 8192 | tf_op jit(solution)/shard_map/psum | solution.py:72
  418.4 2.4 fusion.42
  (6 shorter events, 0.0 us)
Async XLA Ops:
  35.8 6.3 %copy-start.2 = (s32[1024]{0:T(1024)S(1)}, s32[1024]{0:T(1024)}, u32[]{:S(2)}) copy-start(s32[1024]{0:T(1024)} %param.11) | copy-start | bytes 12292
  35.8 127.5 %all-to-all-start.1 = ((bf16[4,5376,256]{2,1,0:T(8,128)(2,1)}), bf16[4,5376,256]{2,1,0:T(8,128)(2,1)}, u32[]{:S(2)}, u32[]{:S(2)}) async-start(bf16[4,5376,256]{2,1,0:T(8,128)(2,1)} %stack.2), calls=%async_computation.1 | async-start | bytes 22020096 | tf_op jit(solution)/shard_map/all_to_all | solution.py:13
  42.0 220.0 %all-gather.2.cloned.1.call-start = ((), (), s32[]{:S(2)}) async-start(), calls=%async_computation.2 | async-start | bytes 13762560 | tf_op jit(solution)/shard_map/all_gather | solution.py:66
  50.5 118.7 %copy-start.3 = (s32[2,5376]{1,0:T(2,128)S(1)}, s32[2,5376]{1,0:T(2,128)}, u32[]{:S(2)}) copy-start(s32[2,5376]{1,0:T(2,128)} %param.12) | copy-start | bytes 129028
  169.3 92.7 %copy-start.1 = (bf16[5376,256]{1,0:T(8,128)(2,1)S(1)}, bf16[5376,256]{1,0:T(8,128)(2,1)}, u32[]{:S(2)}) copy-start(bf16[5376,256]{1,0:T(8,128)(2,1)} %param.8) | copy-start | bytes 8257540
  187.5 223.4 %all-reduce.3.cloned.1.call-start = ((), (), s32[]{:S(2)}) async-start(), calls=%async_computation.3 | async-start | bytes 2097152 | tf_op jit(solution)/shard_map/psum | solution.py:71
  279.7 131.2 %copy-start = (bf16[1024,256]{1,0:T(8,128)(2,1)S(1)}, bf16[1024,256]{1,0:T(8,128)(2,1)}, u32[]{:S(2)}) copy-start(bf16[1024,256]{1,0:T(8,128)(2,1)} %param.7) | copy-start | bytes 1572868
Sparse Core Ops, SparseCore 0:
  187.6 74.3 all-gather.1
  270.3 51.7 all-reduce.2
